TPU v7x, 32 devices: a whole 2x2x4 slice. The times are simulated.
32 devices in a mesh: row: 4 (over x, core), col: 8 (over z, y).
Axes of the slice: x: 2, y: 2, z: 4, core: 2. Of those that a mesh axis runs over, the one named last changes fastest.
Arguments:
- eigvecs: float32 [1024, 1024], P('row', 'col'), may hold values from -6 to 6
- offsets: int32 [1], replicated, may hold values from 0 to 127
- plan: int32 [1, 6], replicated, may hold values from 0 to 7
- refl_v: float32 [8, 255, 128], P('col')
- refl_t: float32 [8, 128, 128], P('col'), as said below
Outputs:
- updated: float32 [1024, 1024], P('row', 'col')
Inputs may be any that keep to these rules, and one draw needn't show every extreme that they name: For each bank entry, I - refl_v refl_t refl_v^T is orthogonal up to rounding.
All inputs are finite; a program needn't handle non-finite values.
Results may differ from a plain program's by a relative error of at most 0.00015.
Values sent between devices are 32-bit elements; how exact they have to be, the bound alone decides.
No kernel may reach another device: no remote copies, remote signals or barrier semaphores. Data moves between devices by JAX's collectives and lax.ppermute only.
A program may use at most 64 MiB of HBM per device.

v0:
```python
import jax
import jax.numpy as jnp
from jax import lax
from jax.sharding import PartitionSpec as P

HIGHEST = lax.Precision.HIGHEST


def apply_one(extended, row_start, vectors, factor, weight):
    span_rows = vectors.shape[0]
    block_rows = lax.dynamic_slice_in_dim(extended, row_start, span_rows, 0)
    inner_prod = jnp.dot(vectors.T, block_rows, precision=HIGHEST)
    scaled = jnp.dot(factor, inner_prod, precision=HIGHEST)
    block_rows = block_rows - weight * jnp.dot(vectors, scaled, precision=HIGHEST)
    return lax.dynamic_update_slice_in_dim(extended, block_rows, row_start, 0)


def on_device(eigvecs, offsets, plan, refl_v, refl_t):
    rows_dev = eigvecs.shape[0]
    band = refl_v.shape[2]
    per_device = rows_dev // band
    row_count = lax.axis_size("row")
    block_total = row_count * per_device - 2
    bank_v, bank_t = (
        lax.all_gather(refl_v, "col", axis=0, tiled=True),
        lax.all_gather(refl_t, "col", axis=0, tiled=True),
    )
    columns = lax.all_to_all(eigvecs, "row", split_axis=1, concat_axis=0, tiled=True)
    first_row = offsets[0]

    def apply_all(index, matrix):
        block_id = plan[0, index]
        row_start = first_row + index * band
        return apply_one(matrix, row_start, bank_v[block_id], bank_t[block_id], 1.0)

    columns = lax.fori_loop(0, block_total, apply_all, columns)
    return lax.all_to_all(columns, "row", split_axis=0, concat_axis=1, tiled=True)


def solution(mesh):
    in_specs = (P("row", "col"), P(), P(), P("col", None, None), P("col", None, None))
    out_specs = P("row", "col")
    return jax.shard_map(
        on_device, mesh=mesh, in_specs=in_specs, out_specs=out_specs, check_vma=False
    )
```

profile of v0, /device:TPU:0, one launch (start us, length us, event | category | flops | bytes accessed | tf_op | source)
XLA Modules:
  0.0 107.6 jit_solution(541290155468602737)
XLA Ops:
  0.0 1.7 %copy.17 = f32[256,128]{0,1:T(8,128)} copy(f32[256,128]{1,0:T(8,128)} %param.7) | data formatting | bytes 262144 | tf_op args[0]
  1.7 4.4 %all-to-all-start = ((f32[256,4,32]{0,2,1:T(8,128)}), f32[256,4,32]{0,2,1:T(8,128)S(1)}, u32[]{:S(2)}, u32[]{:S(2)}) async-start(f32[256,4,32]{0,2,1:T(8,128)} %bitcast.3), calls=%async_computation | async-start | bytes 262144 | tf_op jit(solution)/shard_map/all_to_all | solution.py:28
  6.1 34.2 %all_gather.6 = f32[8,255,128]{2,1,0:T(8,128)S(1)} all-gather(f32[1,255,128]{2,1,0:T(8,128)S(1)} %copy.19), channel_id=1, replica_groups=mesh['row'=4,'col'=8] {'col'}, dimensions={0}, use_global_device_ids=true | all-gather | bytes 1175040 | tf_op jit(solution)/shard_map/all_gather | solution.py:25
  40.3 31.3 %all_gather.7 = f32[8,128,128]{2,1,0:T(8,128)S(1)} all-gather(f32[1,128,128]{2,1,0:T(8,128)S(1)} %copy-done.1), channel_id=1, replica_groups=mesh['row'=4,'col'=8] {'col'}, dimensions={0}, use_global_device_ids=true | all-gather | bytes 589824 | tf_op jit(solution)/shard_map/all_gather | solution.py:26
  71.6 0.6 copy-done.2
  72.3 27.2 %while.13 = (s32[]{:T(128)}, f32[1024,32]{0,1:T(8,128)S(1)}, s32[]{:T(128)}, s32[1,6]{1,0:T(1,128)S(1)}, f32[8,255,128]{2,1,0:T(8,128)S(1)}, /*index=5*/f32[8,12...) while((s32[]{:T(128)}, f32[1024,32]{0,1:T(8,128)S(1)}, ...), condition=%wide.region_1.0_spmd, body=%wide.region_0.0_spmd.sunk | while | flops 31367144 | bytes 556917 | solution.py:36
  72.9 0.6 constant_dynamic-slice_fusion.2
  75.9 0.3 convolution_subtract_fusion.2
  76.2 0.6 dynamic_update_slice.8
  77.5 0.6 constant_dynamic-slice_fusion.2
  80.5 0.3 convolution_subtract_fusion.2
  80.7 0.6 dynamic_update_slice.8
  82.0 0.6 constant_dynamic-slice_fusion.2
  85.0 0.3 convolution_subtract_fusion.2
  85.3 0.6 dynamic_update_slice.8
  86.5 0.6 constant_dynamic-slice_fusion.2
  89.8 0.6 dynamic_update_slice.8
  91.1 0.6 constant_dynamic-slice_fusion.2
  94.3 0.6 dynamic_update_slice.8
  95.6 0.6 constant_dynamic-slice_fusion.2
  98.6 0.3 convolution_subtract_fusion.2
  98.9 0.5 dynamic_update_slice.8
  99.5 7.4 %all_to_all.38 = f32[4,256,32]{1,2,0:T(8,128)S(1)} all-to-all(f32[4,256,32]{1,2,0:T(8,128)S(1)} %bitcast.38), channel_id=1, replica_groups=mesh['row'=4,'col'=8] {'row'}, dimensions={0} | all-to-all | bytes 262144 | tf_op jit(solution)/shard_map/all_to_all | solution.py:37
  106.8 0.8 copy.21
  (23 shorter events, 3.2 us)
Async XLA Ops:
  1.7 4.4 %copy-start = (f32[1,255,128]{2,0,1:T(1,128)S(1)}, f32[1,255,128]{2,0,1:T(1,128)}, u32[]{:S(2)}) copy-start(f32[1,255,128]{2,0,1:T(1,128)} %param.10) | copy-start | bytes 391684
  1.7 69.9 %all-to-all-start = ((f32[256,4,32]{0,2,1:T(8,128)}), f32[256,4,32]{0,2,1:T(8,128)S(1)}, u32[]{:S(2)}, u32[]{:S(2)}) async-start(f32[256,4,32]{0,2,1:T(8,128)} %bitcast.3), calls=%async_computation | async-start | bytes 262144 | tf_op jit(solution)/shard_map/all_to_all | solution.py:28
  6.0 34.2 %copy-start.1 = (f32[1,128,128]{2,1,0:T(8,128)S(1)}, f32[1,128,128]{2,1,0:T(8,128)}, u32[]{:S(2)}) copy-start(f32[1,128,128]{2,1,0:T(8,128)} %param.11) | copy-start | bytes 196612
  71.6 0.7 copy-start.2
where the time goes:
time: 108 us
  blocking collectives  72.9 us (68%)
  loops' own time  15.8 us (15%)
  local copies, waits for them, and re-layouts  10.1 us (9%)
  starting transfers between devices  4.37 us (4%)
  matrix products  4.28 us (4%)
    all_gather x1, blocking collectives, on_device(): lax.all_gather(refl_v, 'col', axis=0, tiled=True)  34.2 us
    all_gather x1, blocking collectives, on_device(): lax.all_gather(refl_t, 'col', axis=0, tiled=True)  31.3 us
    another operation x1, loops' own time, on_device(): columns = lax.fori_loop(0, block_total, apply_all, columns)  15.8 us
    all_to_all x1, blocking collectives, on_device(): lax.all_to_all(columns, 'row', split_axis=0, concat_axis=1, tiled=True)  7.4 us
    all_to_all x1, starting transfers between devices, on_device(): lax.all_to_all(eigvecs, 'row', split_axis=1, concat_axis=0, tiled=True)  4.37 us
    dynamic_update_slice x6, local copies, waits for them, and re-layouts, apply_one(): return lax.dynamic_update_slice_in_dim(extended, block_rows, row_start, 0)  3.52 us
    dynamic_slice x6, local copies, waits for them, and re-layouts, apply_all(): block_id = plan[0, index]  3.51 us
    unnamed x8, local copies, waits for them, and re-layouts  2.33 us
  transfers between devices with their start and end apart: 1, of which 0 were waited for; matrix products, arithmetic and copies ran while one was open for 0% of the time, Pallas kernels for 0%

commit v1 on v0

--- a/solution.py
+++ b/solution.py
@@ -34,7 +34,10 @@
         return apply_one(matrix, row_start, bank_v[block_id], bank_t[block_id], 1.0)
 
     columns = lax.fori_loop(0, block_total, apply_all, columns)
-    return lax.all_to_all(columns, "row", split_axis=0, concat_axis=1, tiled=True)
+    return jnp.concatenate(
+        lax.all_to_all(jnp.stack(jnp.split(columns, lax.axis_size("row"), axis=0)), "row", 0, 0),
+        axis=1,
+    )
 
 
 def solution(mesh):

time: 108 us -> 108 us (level)
  no operation moved by 1% of the time
where the time goes in v1:
time: 108 us
  blocking collectives  72.9 us (68%)
  loops' own time  15.8 us (15%)
  local copies, waits for them, and re-layouts  10.1 us (9%)
  starting transfers between devices  4.37 us (4%)
  matrix products  4.28 us (4%)
    all_gather x1, blocking collectives, on_device(): lax.all_gather(refl_v, 'col', axis=0, tiled=True)  34.2 us
    all_gather x1, blocking collectives, on_device(): lax.all_gather(refl_t, 'col', axis=0, tiled=True)  31.3 us
    another operation x1, loops' own time, on_device(): columns = lax.fori_loop(0, block_total, apply_all, columns)  15.8 us
    all_to_all x1, blocking collectives, on_device(): lax.all_to_all(jnp.stack(jnp.split(columns, lax.axis_size('row'), axis=0)...  7.4 us
    all_to_all x1, starting transfers between devices, on_device(): lax.all_to_all(eigvecs, 'row', split_axis=1, concat_axis=0, tiled=True)  4.37 us
    dynamic_update_slice x6, local copies, waits for them, and re-layouts, apply_one(): return lax.dynamic_update_slice_in_dim(extended, block_rows, row_start, 0)  3.52 us
    dynamic_slice x6, local copies, waits for them, and re-layouts, apply_all(): block_id = plan[0, index]  3.51 us
    unnamed x8, local copies, waits for them, and re-layouts  2.33 us
  transfers between devices with their start and end apart: 1, of which 0 were waited for; matrix products, arithmetic and copies ran while one was open for 0% of the time, Pallas kernels for 0%

profile of v1, /device:TPU:0, one launch (start us, length us, event | category | flops | bytes accessed | tf_op | source)
XLA Modules:
  0.0 107.6 jit_solution(8041815645970762)
XLA Ops:
  0.0 1.7 %copy.16 = f32[256,128]{0,1:T(8,128)} copy(f32[256,128]{1,0:T(8,128)} %param.7) | data formatting | bytes 262144 | tf_op args[0]
  1.7 4.4 %all-to-all-start = ((f32[256,4,32]{0,2,1:T(8,128)}), f32[256,4,32]{0,2,1:T(8,128)S(1)}, u32[]{:S(2)}, u32[]{:S(2)}) async-start(f32[256,4,32]{0,2,1:T(8,128)} %bitcast.3), calls=%async_computation | async-start | bytes 262144 | tf_op jit(solution)/shard_map/all_to_all | solution.py:28
  6.1 34.2 %all_gather.6 = f32[8,255,128]{2,1,0:T(8,128)S(1)} all-gather(f32[1,255,128]{2,1,0:T(8,128)S(1)} %copy.18), channel_id=1, replica_groups=mesh['row'=4,'col'=8] {'col'}, dimensions={0}, use_global_device_ids=true | all-gather | bytes 1175040 | tf_op jit(solution)/shard_map/all_gather | solution.py:25
  40.3 31.3 %all_gather.7 = f32[8,128,128]{2,1,0:T(8,128)S(1)} all-gather(f32[1,128,128]{2,1,0:T(8,128)S(1)} %copy-done.1), channel_id=1, replica_groups=mesh['row'=4,'col'=8] {'col'}, dimensions={0}, use_global_device_ids=true | all-gather | bytes 589824 | tf_op jit(solution)/shard_map/all_gather | solution.py:26
  71.6 0.6 copy-done.2
  72.3 27.2 %while.13 = (s32[]{:T(128)}, f32[1024,32]{0,1:T(8,128)S(1)}, s32[]{:T(128)}, s32[1,6]{1,0:T(1,128)S(1)}, f32[8,255,128]{2,1,0:T(8,128)S(1)}, /*index=5*/f32[8,12...) while((s32[]{:T(128)}, f32[1024,32]{0,1:T(8,128)S(1)}, ...), condition=%wide.region_1.0_spmd, body=%wide.region_0.0_spmd.sunk | while | flops 31367144 | bytes 556917 | solution.py:36
  72.9 0.6 constant_dynamic-slice_fusion.2
  75.9 0.3 convolution_subtract_fusion.2
  76.2 0.6 dynamic_update_slice.8
  77.5 0.6 constant_dynamic-slice_fusion.2
  80.5 0.3 convolution_subtract_fusion.2
  80.7 0.6 dynamic_update_slice.8
  82.0 0.6 constant_dynamic-slice_fusion.2
  85.0 0.3 convolution_subtract_fusion.2
  85.3 0.6 dynamic_update_slice.8
  86.5 0.6 constant_dynamic-slice_fusion.2
  89.8 0.6 dynamic_update_slice.8
  91.1 0.6 constant_dynamic-slice_fusion.2
  94.3 0.6 dynamic_update_slice.8
  95.6 0.6 constant_dynamic-slice_fusion.2
  98.6 0.3 convolution_subtract_fusion.2
  98.9 0.5 dynamic_update_slice.8
  99.5 7.4 %all_to_all.24 = f32[4,256,32]{1,2,0:T(8,128)S(1)} all-to-all(f32[4,256,32]{1,2,0:T(8,128)S(1)} %pad_maximum_fusion), channel_id=1, replica_groups=mesh['row'=4,'col'=8] {'row'}, dimensions={0} | all-to-all | bytes 262144 | tf_op jit(solution)/shard_map/all_to_all | solution.py:38
  106.9 0.8 copy.19
  (24 shorter events, 3.3 us)
Async XLA Ops:
  1.7 4.4 %copy-start = (f32[1,255,128]{2,0,1:T(1,128)S(1)}, f32[1,255,128]{2,0,1:T(1,128)}, u32[]{:S(2)}) copy-start(f32[1,255,128]{2,0,1:T(1,128)} %param.10) | copy-start | bytes 391684
  1.7 69.9 %all-to-all-start = ((f32[256,4,32]{0,2,1:T(8,128)}), f32[256,4,32]{0,2,1:T(8,128)S(1)}, u32[]{:S(2)}, u32[]{:S(2)}) async-start(f32[256,4,32]{0,2,1:T(8,128)} %bitcast.3), calls=%async_computation | async-start | bytes 262144 | tf_op jit(solution)/shard_map/all_to_all | solution.py:28
  6.0 34.2 %copy-start.1 = (f32[1,128,128]{2,1,0:T(8,128)S(1)}, f32[1,128,128]{2,1,0:T(8,128)}, u32[]{:S(2)}) copy-start(f32[1,128,128]{2,1,0:T(8,128)} %param.11) | copy-start | bytes 196612
  71.6 0.7 copy-start.2
